TPU v7x, 256 devices: a whole 4x4x8 slice. The times are simulated.
256 devices in a mesh: pipe: 4 (over z_hi, core), expert: 64 (over x, y, z_lo).
Axes of the slice: x: 4, y: 4, z: 8 (z_hi: 2, z_lo: 4; z = z_hi * 4 + z_lo), core: 2. Of those that a mesh axis runs over, the one named last changes fastest.
Arguments:
- held: bfloat16 [4, 2048, 2048], P('pipe', 'expert'), may hold values from -23 to 23
- fresh: bfloat16 [2048, 2048], P('expert'), may hold values from -23 to 23
- routes: int32 [4, 2048, 2], P('pipe', 'expert'), may hold values from 0 to 7, all different within a row; in each aligned block of 32 rows (0 to 31, 32 to 63, ..., all dimensions but the last counted through in order) at most 16 rows name the same one
- norm_gain: float32 [4, 2048], P('pipe'), may hold values from 0.25 to 1.75
- router: bfloat16 [4, 2048, 8], P('pipe'), may hold values from -0.125 to 0.125
- w_gate: bfloat16 [4, 64, 2048, 896], P('pipe', 'expert'), may hold values from -0.125 to 0.125
- w_up: bfloat16 [4, 64, 2048, 896], P('pipe', 'expert'), may hold values from -0.125 to 0.125
- w_down: bfloat16 [4, 64, 896, 2048], P('pipe', 'expert'), may hold values from -0.0625 to 0.0625
Outputs:
- section_out: bfloat16 [4, 2048, 2048], P('pipe', 'expert')
Inputs may be any that keep to these rules, and one draw needn't show every extreme that they name: `routes`: each token names two different experts; among the 32 tokens of one device at one section no expert is named more than 16 times, and in every draw some device's tokens name one expert exactly 16 times.
All inputs are finite; a program needn't handle non-finite values.
Results may differ from a plain program's by a relative error of at most 0.0045.
Values may be sent and summed in bfloat16 or wider, within the bound.
A program may use at most 128 MiB of HBM per device.

v0:
```python
import jax
import jax.numpy as jnp
from jax import lax
from jax.sharding import PartitionSpec as P


def passed_along(x, axis, by):
    length = lax.axis_size(axis)
    pairs = [(i, i + by) for i in range(length) if 0 <= i + by < length]
    return lax.ppermute(x, axis, pairs)


def per_device(held, fresh, routes, norm_gain, router, w_gate, w_up, w_down):
    tok_rows = fresh.shape[0]
    model_width = fresh.shape[1]
    experts = router.shape[2]
    devices = lax.axis_size("expert")
    shard_count = devices // experts
    capacity = tok_rows // 2
    received = passed_along(held[0], "pipe", 1)
    section_index = lax.axis_index("pipe")
    inputs = jnp.where(section_index == 0, fresh, received)
    values = inputs.astype(jnp.float32)
    mean_square = jnp.mean(values * values, axis=-1, keepdims=True)
    normed = (values * lax.rsqrt(mean_square + 1e-05) * norm_gain[0]).astype(jnp.bfloat16)
    logits = jnp.dot(normed, router[0], preferred_element_type=jnp.float32)
    chosen = routes[0]
    expert_ids = jnp.arange(experts, dtype=jnp.int32)
    token_hits = (chosen[:, :, None] == expert_ids[None, None, :]).astype(jnp.float32)
    picked_logits = jnp.sum(token_hits * logits[:, None, :], axis=2)
    shares = jnp.stack(
        [
            jax.nn.sigmoid(picked_logits[:, 0] - picked_logits[:, 1]),
            jax.nn.sigmoid(picked_logits[:, 1] - picked_logits[:, 0]),
        ],
        axis=1,
    )
    flat_choice = chosen.reshape(-1)
    onehot = (flat_choice[:, None] == expert_ids[None, :]).astype(jnp.int32)
    rank_table = jnp.cumsum(onehot, axis=0) - 1
    slot_index = jnp.sum(onehot * rank_table, axis=1)
    target = flat_choice * capacity + slot_index
    slot_ids = jnp.arange(experts * capacity, dtype=jnp.int32)
    placing = (target[:, None] == slot_ids[None, :]).astype(jnp.bfloat16)
    placing_tok = jnp.sum(placing.reshape(tok_rows, 2, experts * capacity), axis=1)
    buffer = jnp.dot(placing_tok.T, normed, preferred_element_type=jnp.float32).astype(jnp.bfloat16)
    gate_matrix = w_gate[0, 0]
    up_matrix = w_up[0, 0]
    down_matrix = w_down[0, 0]
    outgoing = jnp.broadcast_to(
        buffer.reshape(experts, 1, capacity, model_width),
        (experts, shard_count, capacity, model_width),
    )
    outgoing = outgoing.reshape(devices, capacity, model_width)
    row_block = lax.all_to_all(outgoing, "expert", split_axis=0, concat_axis=0, tiled=True)
    flat_rows = row_block.reshape(-1, model_width)
    gate_proj = jnp.dot(flat_rows, gate_matrix, preferred_element_type=jnp.float32)
    up_proj = jnp.dot(flat_rows, up_matrix, preferred_element_type=jnp.float32)
    hidden = (jax.nn.silu(gate_proj) * up_proj).astype(jnp.bfloat16)
    partial_value = jnp.dot(hidden, down_matrix, preferred_element_type=jnp.float32).astype(
        jnp.bfloat16
    )
    came_back = lax.all_to_all(
        partial_value.reshape(row_block.shape), "expert", split_axis=0, concat_axis=0, tiled=True
    )
    expert_out = jnp.sum(
        came_back.reshape(experts, shard_count, capacity, model_width).astype(jnp.float32), axis=1
    ).astype(jnp.bfloat16)
    picked = jnp.dot(
        placing,
        expert_out.reshape(experts * capacity, model_width),
        preferred_element_type=jnp.float32,
    )
    picked = picked.reshape(tok_rows, 2, model_width)
    branch = shares[:, 0, None] * picked[:, 0] + shares[:, 1, None] * picked[:, 1]
    section_out = (values + branch).astype(jnp.bfloat16)
    return section_out[None]


def solution(mesh):
    in_specs = (
        P("pipe", "expert", None),
        P("expert", None),
        P("pipe", "expert", None),
        P("pipe", None),
        P("pipe", None, None),
        P("pipe", "expert", None, None),
        P("pipe", "expert", None, None),
        P("pipe", "expert", None, None),
    )
    out_specs = P("pipe", "expert", None)
    return jax.shard_map(
        per_device, mesh=mesh, in_specs=in_specs, out_specs=out_specs, check_vma=False
    )
```

profile of v0, /device:TPU:1, one launch (start us, length us, event | category | flops | bytes accessed | tf_op | source)
XLA Modules:
  0.0 238.6 jit_solution(10498512450615917000)
XLA Ops:
  0.0 0.0 copy-start
  0.0 10.3 %collective-permute-start = (bf16[32,2048]{1,0:T(8,128)(2,1)}, bf16[32,2048]{1,0:T(8,128)(2,1)S(1)}, u32[]{:S(2)}, u32[]{:S(2)}) collective-permute-start(bf16[32,2048]{1,0:T(8,128)(2,1)} %bitcast.68), channel_id=1, source_target_pairs={{0,64},{64,128},{128,192},{1,65},{65,129},{129,193},{2,66},{66,130... | collective-permute-start | bytes 393224 | tf_op jit(solution)/shard_map/ppermute | solution.py:10
  10.3 0.8 copy.19
  11.1 0.1 eq.74
  11.2 0.1 fusion.19
  11.3 0.1 reduce_window_sum.11
  11.4 0.2 select_reduce_fusion
  11.6 0.1 reduce_sum.56
  11.7 0.1 copy.20
  11.7 0.7 multiply_add_fusion
  12.4 0.1 fusion.24
  12.5 0.1 collective-permute-done
  12.6 0.2 fusion.7
  12.7 1.0 convolution_convert_fusion.1
  13.8 0.5 broadcast_in_dim.7
  14.3 0.0 copy-start.3
  14.3 103.5 %all_to_all.10 = bf16[64,16,2048]{2,1,0:T(8,128)(2,1)S(1)} all-to-all(bf16[64,16,2048]{2,1,0:T(8,128)(2,1)S(1)} %bitcast.59), channel_id=1, replica_groups=mesh['pipe'=4,'expert'=64] {'expert'}, dimensions={0} | all-to-all | bytes 8388608 | tf_op jit(solution)/shard_map/all_to_all | solution.py:55
  117.8 0.0 copy-done.3
  117.8 0.0 copy-start.4
  117.8 4.5 %fusion.1 = f32[1024,896]{1,0:T(8,128)S(1)} fusion(bf16[1024,2048]{1,0:T(8,128)(2,1)S(1)} %bitcast.61, bf16[1,1,2048,896]{3,2,1,0:T(8,128)(2,1)S(1)} %copy-done.3), kind=kOutput, calls=%fused_computation.3 | convolution fusion | flops 3758096384 | bytes 11534336 | tf_op jit(solution)/shard_map/dot_general | solution.py:58
  122.3 0.0 copy-done.4
  122.3 0.0 copy-start.5
  122.3 4.8 %multiply_convert_fusion = bf16[1024,896]{1,0:T(8,128)(2,1)S(1)} fusion(f32[1024,896]{1,0:T(8,128)S(1)} %fusion.1, bf16[1024,2048]{1,0:T(8,128)(2,1)S(1)} %bitcast.62, bf16[1,1,2048,896]{3,2,1,0:T(8,128)(2,1)S(1)} %copy-done.4), kind=kOutput, calls=%fused_computation.7 | convolution fusion | flops 3763601408 | bytes 13369344 | tf_op jit(solution)/shard_map/dot_general | solution.py:57
  127.1 0.0 copy-done.5
  127.1 6.1 %convolution_convert_fusion = bf16[1024,2048]{1,0:T(8,128)(2,1)} fusion(bf16[1024,896]{1,0:T(8,128)(2,1)S(1)} %multiply_convert_fusion, bf16[1,1,896,2048]{3,2,1,0:T(8,128)(2,1)S(1)} %copy-done.5), kind=kOutput, calls=%fused_computation.1 | convolution fusion | flops 3760193536 | bytes 9699328 | tf_op jit(solution)/shard_map/dot_general | solution.py:60
  133.1 0.0 copy-start.2
  133.2 0.0 copy-start.1
  133.2 5.8 %all-to-all-start.1 = ((bf16[64,16,2048]{2,1,0:T(8,128)(2,1)}), bf16[64,16,2048]{2,1,0:T(8,128)(2,1)}, u32[]{:S(2)}, u32[]{:S(2)}) async-start(bf16[64,16,2048]{2,1,0:T(8,128)(2,1)} %bitcast.60), calls=%async_computation.1 | async-start | bytes 8388608 | tf_op jit(solution)/shard_map/all_to_all | solution.py:63
  139.0 0.0 copy-done
  139.0 0.0 copy-done.2
  139.0 0.2 fusion.16
  139.2 0.0 copy-done.1
  139.2 95.4 %all-to-all-done.1 = bf16[64,16,2048]{2,1,0:T(8,128)(2,1)} async-done(((bf16[64,16,2048]{2,1,0:T(8,128)(2,1)}), bf16[64,16,2048]{2,1,0:T(8,128)(2,1)}, u32[]{:S(2)}, u32[]{:S(2)}) %all-to-all-start.1) | async-done | bytes 4194336 | tf_op jit(solution)/shard_map/all_to_all | solution.py:63
  234.6 2.9 %bitcast_reduce_fusion = bf16[8,16,2048]{2,1,0:T(8,128)(2,1)S(1)} fusion(bf16[64,16,2048]{2,1,0:T(8,128)(2,1)} %all-to-all-done.1), kind=kLoop, calls=%fused_computation | loop fusion | flops 1835008 | bytes 4718592 | tf_op jit(solution)/shard_map/reduce_sum | solution.py:66
  237.5 0.3 fusion.21
  237.8 0.8 fusion.14
  (3 shorter events, 0.0 us)
Async XLA Ops:
  0.0 139.0 %copy-start = (bf16[1,2048,8]{1,2,0:T(8,128)(2,1)S(1)}, bf16[1,2048,8]{1,2,0:T(8,128)(2,1)}, u32[]{:S(2)}) copy-start(bf16[1,2048,8]{1,2,0:T(8,128)(2,1)} %param.12) | copy-start | bytes 98308
  0.0 12.6 %collective-permute-start = (bf16[32,2048]{1,0:T(8,128)(2,1)}, bf16[32,2048]{1,0:T(8,128)(2,1)S(1)}, u32[]{:S(2)}, u32[]{:S(2)}) collective-permute-start(bf16[32,2048]{1,0:T(8,128)(2,1)} %bitcast.68), channel_id=1, source_target_pairs={{0,64},{64,128},{128,192},{1,65},{65,129},{129,193},{2,66},{66,130... | collective-permute-start | bytes 393224 | tf_op jit(solution)/shard_map/ppermute | solution.py:10
  14.3 103.5 %copy-start.3 = (bf16[1,1,2048,896]{3,2,1,0:T(8,128)(2,1)S(1)}, bf16[1,1,2048,896]{3,2,1,0:T(8,128)(2,1)}, u32[]{:S(2)}) copy-start(bf16[1,1,2048,896]{3,2,1,0:T(8,128)(2,1)} %param.14) | copy-start | bytes 11010052
  117.8 4.5 %copy-start.4 = (bf16[1,1,2048,896]{3,2,1,0:T(8,128)(2,1)S(1)}, bf16[1,1,2048,896]{3,2,1,0:T(8,128)(2,1)}, u32[]{:S(2)}) copy-start(bf16[1,1,2048,896]{3,2,1,0:T(8,128)(2,1)} %param.13) | copy-start | bytes 11010052
  122.3 4.8 %copy-start.5 = (bf16[1,1,896,2048]{3,2,1,0:T(8,128)(2,1)S(1)}, bf16[1,1,896,2048]{3,2,1,0:T(8,128)(2,1)}, u32[]{:S(2)}) copy-start(bf16[1,1,896,2048]{3,2,1,0:T(8,128)(2,1)} %param.15) | copy-start | bytes 11010052
  133.1 5.8 %copy-start.2 = (f32[1,2048]{1,0:T(1,128)S(1)}, f32[1,2048]{1,0:T(1,128)}, u32[]{:S(2)}) copy-start(f32[1,2048]{1,0:T(1,128)} %param.11) | copy-start | bytes 24580
  133.2 6.0 %copy-start.1 = (s32[1,32,2]{1,2,0:T(2,128)S(1)}, s32[1,32,2]{1,2,0:T(2,128)}, u32[]{:S(2)}) copy-start(s32[1,32,2]{1,2,0:T(2,128)} %param.10) | copy-start | bytes 772
  133.2 101.5 %all-to-all-start.1 = ((bf16[64,16,2048]{2,1,0:T(8,128)(2,1)}), bf16[64,16,2048]{2,1,0:T(8,128)(2,1)}, u32[]{:S(2)}, u32[]{:S(2)}) async-start(bf16[64,16,2048]{2,1,0:T(8,128)(2,1)} %bitcast.60), calls=%async_computation.1 | async-start | bytes 8388608 | tf_op jit(solution)/shard_map/all_to_all | solution.py:63
where the time goes:
time: 239 us
  blocking collectives  103 us (43%)
  waiting for transfers between devices  95.4 us (40%)
  matrix products  16.9 us (7%)
  starting transfers between devices  16.1 us (7%)
  other arithmetic  4.99 us (2%)
    all_to_all x1, blocking collectives, per_device(): lax.all_to_all(outgoing, 'expert', split_axis=0, concat_axis=0, tiled=True)  103 us
    all_to_all x1, waiting for transfers between devices, per_device(): lax.all_to_all(partial_value.reshape(row_block.shape), 'expert', split_ax...  95.4 us
    ppermute x1, starting transfers between devices, passed_along(): return lax.ppermute(x, axis, pairs)  10.3 us
    dot_general x1, matrix products, per_device(): jnp.dot(hidden, down_matrix, preferred_element_type=jnp.float32)  6.07 us
    all_to_all x1, starting transfers between devices, per_device(): lax.all_to_all(partial_value.reshape(row_block.shape), 'expert', split_ax...  5.79 us
  transfers between devices with their start and end apart: 2, of which 2 were waited for; matrix products, arithmetic and copies ran while one was open for 1% of the time, Pallas kernels for 0%

commit v1 on v0

v1 whole, which is shorter than its diff:
```python
import functools

import jax
import jax.numpy as jnp
from jax import lax
from jax.experimental import pallas as pl
from jax.experimental.pallas import tpu as pltpu
from jax.sharding import PartitionSpec as P

MESH = pl.DeviceIdType.MESH
SIDE = 4
EXPERTS = 8
CAP = 16
TOK = 32
META = 128
BLOCK = SIDE * CAP
F32 = jnp.float32
BF16 = jnp.bfloat16


def passed_along(x, axis, by):
    length = lax.axis_size(axis)
    pairs = [(i, i + by) for i in range(length) if 0 <= i + by < length]
    return lax.ppermute(x, axis, pairs)


def z_partner(z, k):
    return (z, z + 1 - 2 * (z % 2), (z + 2) % SIDE, 3 - z)[k]


def moe_kernel(
    ext_ref, inputs_ref, gate_ref, up_ref, down_ref, out_ref,
    dense, slots, rows, parts, back, merged, spread, sums, final, hidden, w_in, w_out,
    z_send, z_recv, d_send, d_recv, f_send, f_recv,
    rf_send, rf_recv, rd_send, rd_recv, rz_send, rz_recv, w_sem,
):
    me = lax.axis_index("expert")
    x, y, z = me // 16, (me // 4) % 4, me % 4
    width = inputs_ref.shape[1]
    tiles = gate_ref.shape[1] // 128

    def at(nx, ny, nz):
        return {"expert": nx * 16 + ny * 4 + nz}

    def along(axis, by):
        if axis == "x":
            return at((x + by + SIDE) % SIDE, y, z)
        return at(x, (y + by + SIDE) % SIDE, z)

    inner = ("x", "y", "y", "x")
    outer = ("y", "x", "x", "y")

    barrier = pltpu.get_barrier_semaphore()
    for d in range(1, SIDE):
        for who in (along("x", d), along("y", d), at(x, y, z_partner(z, d))):
            pl.semaphore_signal(barrier, inc=1, device_id=who, device_id_type=MESH)
    pl.semaphore_wait(barrier, 9)

    def remote(src, dst, send, recv, who):
        return pltpu.make_async_remote_copy(
            src_ref=src, dst_ref=dst, send_sem=send, recv_sem=recv, device_id=who, device_id_type=MESH
        )

    z_copy = {
        k: remote(ext_ref, dense.at[k, 0], z_send.at[k], z_recv.at[k], at(x, y, z_partner(z, k)))
        for k in range(1, SIDE)
    }

    def d_copies(k):
        src = ext_ref if k == 0 else dense.at[k, 0]
        return [
            remote(src, dense.at[k, d], d_send.at[k, d], d_recv.at[k, d], along(inner[k], d))
            for d in range(1, SIDE)
        ]

    def f_copies(k):
        return [
            remote(slots.at[k, d - 1], rows.at[k, d], f_send.at[k, d], f_recv.at[k, d], along(outer[k], d))
            for d in range(1, SIDE)
        ]

    def rf_copies(k):
        return [
            remote(parts.at[k, d - 1], back.at[k, d], rf_send.at[k, d], rf_recv.at[k, d], along(outer[k], -d))
            for d in range(1, SIDE)
        ]

    def rd_copies(k):
        return [
            remote(merged.at[k, d], spread.at[k, d - 1], rd_send.at[k, d], rd_recv.at[k, d], along(inner[k], -d))
            for d in range(1, SIDE)
        ]

    rz_copy = {
        k: remote(sums.at[k], final.at[k], rz_send.at[k], rz_recv.at[k], at(x, y, z_partner(z, k)))
        for k in range(1, SIDE)
    }
    steps = {}

    def start(name, k, copies):
        steps[name, k] = copies
        for copy in copies:
            copy.start()

    def arrive(name, k):
        for copy in steps[name, k]:
            copy.wait_recv()

    def lane_expert(k, lane):
        block = lane // BLOCK
        if outer[k] == "y":
            return 2 * x + ((y + block) % SIDE) // 2
        return 2 * ((x + block) % SIDE) + y // 2

    def compact(k):
        tok = dense[k].reshape(SIDE * TOK, width + META)
        meta = tok[:, width:]
        lane = lax.broadcasted_iota(jnp.int32, (SIDE * BLOCK, META), 0)
        col = lax.broadcasted_iota(jnp.int32, (SIDE * BLOCK, META), 1)
        pick = (col == lane_expert(k, lane)).astype(F32).astype(BF16)
        found = lax.dot_general(pick, meta, (((1,), (1,)), ((), ())), preferred_element_type=F32)
        lane = lax.broadcasted_iota(jnp.int32, (SIDE * BLOCK, SIDE * TOK), 0)
        token = lax.broadcasted_iota(jnp.int32, (SIDE * BLOCK, SIDE * TOK), 1)
        want = (lane % CAP + 1).astype(F32)
        near = (lane % BLOCK) // CAP == token // TOK
        placing = jnp.where((found == want) & near, 1.0, 0.0).astype(BF16)
        moved = jnp.dot(placing, tok[:, :width], preferred_element_type=F32).astype(BF16)
        rows[k, 0] = moved[:BLOCK]
        slots[k] = moved[BLOCK:].reshape(SIDE - 1, BLOCK, width)

    def experts(k):
        taken = rows[k].reshape(SIDE * BLOCK, width)

        def first(n, carry):
            cols = pl.ds(pl.multiple_of(n * 256, 256), 256)
            both = jnp.dot(taken, w_in[:, cols], preferred_element_type=F32)
            gate, up = both[:, :128], both[:, 128:]
            value = gate / (1.0 + jnp.exp(-gate)) * up
            hidden[:, pl.ds(pl.multiple_of(n * 128, 128), 128)] = value.astype(BF16)
            return carry

        lax.fori_loop(0, tiles, first, 0)

        def second(n, carry):
            cols = pl.ds(pl.multiple_of(n * 256, 256), 256)
            value = jnp.dot(hidden[...], w_out[:, cols], preferred_element_type=F32).astype(BF16)
            back[k, 0, :, cols] = value[:BLOCK]
            for d in range(1, SIDE):
                parts[k, d - 1, :, cols] = value[d * BLOCK : (d + 1) * BLOCK]
            return carry

        lax.fori_loop(0, width // 256, second, 0)

    def merge(k):
        meta = dense[k, :, :, pl.ds(width, META)].reshape(SIDE * TOK, META)
        col = lax.broadcasted_iota(jnp.int32, (META, SIDE * BLOCK), 0)
        lane = lax.broadcasted_iota(jnp.int32, (META, SIDE * BLOCK), 1)
        mine = lane_expert(k, lane)

        def look(shift):
            pick = (col == mine + shift).astype(F32).astype(BF16)
            return jnp.dot(meta, pick, preferred_element_type=F32)

        token = lax.broadcasted_iota(jnp.int32, (SIDE * TOK, SIDE * BLOCK), 0)
        lane = lax.broadcasted_iota(jnp.int32, (SIDE * TOK, SIDE * BLOCK), 1)
        want = (lane % CAP + 1).astype(F32)
        near = (lane % BLOCK) // CAP == token // TOK
        match = (look(0) == want) & near
        high = jnp.where(match, look(EXPERTS), 0.0).astype(BF16)
        low = jnp.where(match, look(2 * EXPERTS), 0.0).astype(BF16)
        came = back[k].reshape(SIDE * BLOCK, width)
        total = jnp.dot(high, came, preferred_element_type=F32) + jnp.dot(low, came, preferred_element_type=F32)
        merged[k] = total.astype(BF16).reshape(SIDE, TOK, width)

    def gather_sum(k):
        total = merged[k, 0].astype(F32)
        for d in range(1, SIDE):
            total = total + spread[k, d - 1].astype(F32)
        sums[k] = total.astype(BF16)

    weights = [pltpu.make_async_copy(down_ref, w_out, w_sem.at[2 * tiles])]
    for n in range(tiles):
        for j, ref in enumerate((gate_ref, up_ref)):
            weights.append(
                pltpu.make_async_copy(
                    ref.at[:, pl.ds(n * 128, 128)],
                    w_in.at[:, pl.ds(n * 256 + j * 128, 128)],
                    w_sem.at[2 * n + j],
                )
            )

    order = (0, 2, 3, 1)
    start("d", 0, d_copies(0))
    for k in order[1:]:
        start("z", k, [z_copy[k]])
    for copy in weights:
        copy.start()
    dense[0, 0] = ext_ref[...]

    def dense_on(k):
        arrive("z", k)
        start("d", k, d_copies(k))

    def dispatch(k):
        arrive("d", k)
        compact(k)
        start("f", k, f_copies(k))

    def compute(k):
        arrive("f", k)
        experts(k)
        start("rf", k, rf_copies(k))

    def combine(k):
        arrive("rf", k)
        merge(k)
        start("rd", k, rd_copies(k))

    def collect(k):
        arrive("rd", k)
        gather_sum(k)
        if k:
            start("rz", k, [rz_copy[k]])

    dense_on(2)
    dispatch(0)
    dense_on(3)
    dispatch(2)
    dense_on(1)
    dispatch(3)
    dispatch(1)
    for copy in weights:
        copy.wait()
    compute(0)
    compute(2)
    compute(3)
    combine(0)
    compute(1)
    combine(2)
    collect(0)
    collect(2)
    combine(3)
    combine(1)
    collect(3)
    collect(1)
    total = inputs_ref[...].astype(F32) + sums[0].astype(F32)
    for k in order[1:]:
        arrive("rz", k)
        total = total + final[k].astype(F32)
    out_ref[...] = total.astype(BF16)
    for copies in steps.values():
        for copy in copies:
            copy.wait_send()


def run_layer(ext, inputs, gate, up, down):
    tok, width = inputs.shape
    hid = gate.shape[1]
    vmem = pl.BlockSpec(memory_space=pltpu.VMEM)
    hbm = pl.BlockSpec(memory_space=pl.ANY)
    dma = pltpu.SemaphoreType.DMA
    pairs = [dma((SIDE,)), dma((SIDE,))]
    grids = [dma((SIDE, SIDE)), dma((SIDE, SIDE))]
    return pl.pallas_call(
        moe_kernel,
        out_shape=jax.ShapeDtypeStruct((tok, width), BF16),
        in_specs=[vmem, vmem, hbm, hbm, hbm],
        out_specs=vmem,
        scratch_shapes=[
            pltpu.VMEM((SIDE, SIDE, tok, width + META), BF16),
            pltpu.VMEM((SIDE, SIDE - 1, BLOCK, width), BF16),
            pltpu.VMEM((SIDE, SIDE, BLOCK, width), BF16),
            pltpu.VMEM((SIDE, SIDE - 1, BLOCK, width), BF16),
            pltpu.VMEM((SIDE, SIDE, BLOCK, width), BF16),
            pltpu.VMEM((SIDE, SIDE, tok, width), BF16),
            pltpu.VMEM((SIDE, SIDE - 1, tok, width), BF16),
            pltpu.VMEM((SIDE, tok, width), BF16),
            pltpu.VMEM((SIDE, tok, width), BF16),
            pltpu.VMEM((SIDE * BLOCK, hid), BF16),
            pltpu.VMEM((width, 2 * hid), BF16),
            pltpu.VMEM((hid, width), BF16),
        ]
        + pairs + grids + grids + grids + grids + pairs
        + [dma((2 * (hid // 128) + 1,))],
        compiler_params=pltpu.CompilerParams(
            collective_id=0, has_side_effects=True, vmem_limit_bytes=60 * 1024 * 1024
        ),
        name="moe_relay",
    )(ext, inputs, gate, up, down)


def per_device(held, fresh, routes, norm_gain, router, w_gate, w_up, w_down):
    received = passed_along(held[0], "pipe", 1)
    section_index = lax.axis_index("pipe")
    inputs = jnp.where(section_index == 0, fresh, received)
    values = inputs.astype(F32)
    mean_square = jnp.mean(values * values, axis=-1, keepdims=True)
    normed = (values * lax.rsqrt(mean_square + 1e-05) * norm_gain[0]).astype(BF16)
    logits = jnp.dot(normed, router[0], preferred_element_type=F32)
    chosen = routes[0]
    expert_ids = jnp.arange(EXPERTS, dtype=jnp.int32)
    hits = chosen[:, :, None] == expert_ids[None, None, :]
    picked = jnp.sum(hits.astype(F32) * logits[:, None, :], axis=2)
    share = jax.nn.sigmoid(picked - picked[:, ::-1])
    weight = jnp.sum(hits.astype(F32) * share[:, :, None], axis=1)
    high = lax.reduce_precision(weight, 8, 7)
    low = weight - high
    hit = jnp.any(hits, axis=1).astype(F32)
    earlier = jnp.tril(jnp.ones((TOK, TOK), F32))
    slot = hit * jnp.dot(earlier, hit, preferred_element_type=F32)
    pad = jnp.zeros((TOK, META - 3 * EXPERTS), BF16)
    ext = jnp.concatenate(
        [normed, slot.astype(BF16), high.astype(BF16), low.astype(BF16), pad], axis=1
    )
    out = run_layer(ext, inputs, w_gate[0, 0], w_up[0, 0], w_down[0, 0])
    return out[None]


def solution(mesh):
    in_specs = (
        P("pipe", "expert", None),
        P("expert", None),
        P("pipe", "expert", None),
        P("pipe", None),
        P("pipe", None, None),
        P("pipe", "expert", None, None),
        P("pipe", "expert", None, None),
        P("pipe", "expert", None, None),
    )
    out_specs = P("pipe", "expert", None)
    return jax.shard_map(
        per_device, mesh=mesh, in_specs=in_specs, out_specs=out_specs, check_vma=False
    )
```

time: 239 us -> 111 us (0.46)
  blocking collectives: 103 us -> 0 us
  waiting for transfers between devices: 95.4 us -> 1.33 us
  Pallas kernels: 0 us -> 92 us
  matrix products: 16.9 us -> 0.26 us
  starting transfers between devices: 16.1 us -> 10.3 us
    all_to_all x1 -> x0, blocking collectives: 103 us -> none  [per_device(): lax.all_to_all(outgoing, 'expert', split_axis=0, concat_axis=0, tiled=True)]
    all_to_all x1 -> x0, waiting for transfers between devices: 95.4 us -> none  [per_device(): lax.all_to_all(partial_value.reshape(row_block.shape), 'expert', split_ax...]
    pallas_call x0 -> x1, Pallas kernels: none -> 92 us  [run_layer(): pl.pallas_call(moe_kernel, out_shape=jax.ShapeDtypeStruct((tok, width), B...]
    dot_general x6 -> x2, matrix products: 16.9 us -> 0.26 us  [the longest x1 0.14 us: per_device(): logits = jnp.dot(normed, router[0], preferred_element_type=F32)]
    all_to_all x1 -> x0, starting transfers between devices: 5.79 us -> none  [per_device(): lax.all_to_all(partial_value.reshape(row_block.shape), 'expert', split_ax...]
  transfers between devices with their start and end apart: 2 -> 1, of which waited for: 2 -> 1; matrix products, arithmetic and copies ran while one was open for 1% -> 1% of each run, Pallas kernels for 0% -> 0%
where the time goes in v1:
time: 111 us; the launch traced here: 110 us
  Pallas kernels  92 us (83%)
  starting transfers between devices  10.3 us (9%)
  other arithmetic  3.12 us (3%)
  local copies, waits for them, and re-layouts  2.59 us (2%)
  waiting for transfers between devices  1.33 us (1%)
    pallas_call x1, Pallas kernels, run_layer(): pl.pallas_call(moe_kernel, out_shape=jax.ShapeDtypeStruct((tok, width), B...  92 us
    ppermute x1, starting transfers between devices, passed_along(): return lax.ppermute(x, axis, pairs)  10.3 us
  transfers between devices with their start and end apart: 1, of which 1 were waited for; matrix products, arithmetic and copies ran while one was open for 1% of the time, Pallas kernels for 0%

profile of v1, /device:TPU:1, one launch (start us, length us, event | category | flops | bytes accessed | tf_op | source)
XLA Modules:
  0.0 109.7 jit_solution(10506684873555462049)
XLA Ops:
  0.0 0.0 copy-start
  0.0 10.3 %collective-permute-start = (bf16[32,2048]{1,0:T(8,128)(2,1)}, bf16[32,2048]{1,0:T(8,128)(2,1)S(1)}, u32[]{:S(2)}, u32[]{:S(2)}) collective-permute-start(bf16[32,2048]{1,0:T(8,128)(2,1)} %bitcast.20), channel_id=1, source_target_pairs={{0,64},{64,128},{128,192},{1,65},{65,129},{129,193},{2,66},{66,130... | collective-permute-start | bytes 393224 | tf_op jit(solution)/shard_map/ppermute | solution.py:24
  10.3 0.7 fusion.9
  11.0 0.1 copy.16
  11.1 0.1 fusion
  11.2 1.3 %collective-permute-done = bf16[32,2048]{1,0:T(8,128)(2,1)S(1)} collective-permute-done((bf16[32,2048]{1,0:T(8,128)(2,1)}, bf16[32,2048]{1,0:T(8,128)(2,1)S(1)}, u32[]{:S(2)}, u32[]{:S(2)}) %collective-permute-start) | collective-permute-done | bytes 131104 | tf_op jit(solution)/shard_map/ppermute | solution.py:24
  12.6 0.2 fusion.1
  12.7 0.0 copy-start.1
  12.7 0.8 fusion.3
  13.6 0.0 copy-done
  13.6 0.1 fusion.4
  13.7 0.7 select_reduce_fusion.1
  14.5 0.7 select_reduce_fusion
  15.2 0.1 copy.19
  15.3 0.1 copy.18
  15.4 0.7 concatenate.3.ext_ref
  16.1 0.0 copy-done.1
  16.1 92.0 %moe_relay.1 = bf16[32,2048]{1,0:T(8,128)(2,1)} custom-call(bf16[32,2176]{1,0:T(8,128)(2,1)} %concatenate.3.ext_ref, bf16[32,2048]{1,0:T(8,128)(2,1)} %copy-done.1, bf16[2048,896]{1,0:T(8,128)(2,1)} %bitcast.12, bf16[2048,896]{1,0:T(8,128)(2,1)} %bitcast.13, bf16[896,2048]{1,0:T(8,128)(2,1)} %bitcast.14), custom_call_target="tpu_custom_call" | custom-call | tf_op jit(solution)/shard_map/moe_relay/pallas_call | solution.py:264
  108.1 1.6 %copy.23 = bf16[1,32,2048]{2,1,0:T(8,128)(2,1)} copy(bf16[1,32,2048]{2,1,0:T(8,128)(2,1)} %bitcast.15) | data formatting | bytes 262144
  (6 shorter events, 0.1 us)
Async XLA Ops:
  0.0 13.6 %copy-start = (bf16[1,2048,8]{1,2,0:T(8,128)(2,1)S(1)}, bf16[1,2048,8]{1,2,0:T(8,128)(2,1)}, u32[]{:S(2)}) copy-start(bf16[1,2048,8]{1,2,0:T(8,128)(2,1)} %param.12) | copy-start | bytes 98308
  0.0 12.6 %collective-permute-start = (bf16[32,2048]{1,0:T(8,128)(2,1)}, bf16[32,2048]{1,0:T(8,128)(2,1)S(1)}, u32[]{:S(2)}, u32[]{:S(2)}) collective-permute-start(bf16[32,2048]{1,0:T(8,128)(2,1)} %bitcast.20), channel_id=1, source_target_pairs={{0,64},{64,128},{128,192},{1,65},{65,129},{129,193},{2,66},{66,130... | collective-permute-start | bytes 393224 | tf_op jit(solution)/shard_map/ppermute | solution.py:24
  12.7 3.4 %copy-start.1 = (bf16[32,2048]{1,0:T(8,128)(2,1)}, bf16[32,2048]{1,0:T(8,128)(2,1)S(1)}, u32[]{:S(2)}) copy-start(bf16[32,2048]{1,0:T(8,128)(2,1)S(1)} %get-tuple-element.6.inputs_ref) | copy-start | bytes 393220

commit v2 on v1

v2 whole, which is shorter than its diff:
```python
import functools

import jax
import jax.numpy as jnp
from jax import lax
from jax.experimental import pallas as pl
from jax.experimental.pallas import tpu as pltpu
from jax.sharding import PartitionSpec as P

MESH = pl.DeviceIdType.MESH
SIDE = 4
EXPERTS = 8
CAP = 16
TOK = 32
META = 128
BLOCK = SIDE * CAP
F32 = jnp.float32
BF16 = jnp.bfloat16


def z_partner(z, k):
    return (z, z + 1 - 2 * (z % 2), (z + 2) % SIDE, 3 - z)[k]


def moe_kernel(
    held_ref, fresh_ref, routes_ref, gain_ref, router_ref, gate_ref, up_ref, down_ref, out_ref,
    inputs, dense, slots, rows, parts, back, merged, spread, sums, final, pair_parts, pair_merged, hidden, w_in, w_out,
    z_send, z_recv, d_send, d_recv, f_send, f_recv,
    rf_send, rf_recv, rd_send, rd_recv, rz_send, rz_recv, q_send, q_recv, p_send, p_recv, w_sem,
):
    me = lax.axis_index("expert")
    stage, stages = lax.axis_index("pipe"), lax.axis_size("pipe")
    x, y, z = me // 16, (me // 4) % 4, me % 4
    width = fresh_ref.shape[1]
    tiles = gate_ref.shape[1] // 128

    def at(nx, ny, nz):
        return {"expert": nx * 16 + ny * 4 + nz}

    def along(axis, by):
        if axis == "x":
            return at((x + by + SIDE) % SIDE, y, z)
        return at(x, (y + by + SIDE) % SIDE, z)

    inner = ("x", "x", "y", "y")
    outer = ("y", "y", "x", "x")

    def section(by):
        return {"pipe": stage + by, "expert": me}

    barrier = pltpu.get_barrier_semaphore()

    @pl.when(stage < stages - 1)
    def _():
        pl.semaphore_signal(barrier, inc=1, device_id=section(1), device_id_type=MESH)

    @pl.when(stage > 0)
    def _():
        pl.semaphore_signal(barrier, inc=1, device_id=section(-1), device_id_type=MESH)

    for d in range(1, SIDE):
        for who in (along("x", d), along("y", d), at(x, y, z_partner(z, d))):
            pl.semaphore_signal(barrier, inc=1, device_id=who, device_id_type=MESH)
    before, after = (stage + stages - 1) // stages, (2 * stages - 2 - stage) // stages
    pl.semaphore_wait(barrier, 9 + before + after)

    def remote(src, dst, send, recv, who):
        return pltpu.make_async_remote_copy(
            src_ref=src, dst_ref=dst, send_sem=send, recv_sem=recv, device_id=who, device_id_type=MESH
        )

    relay = remote(held_ref, inputs, p_send.at[0], p_recv.at[0], section(1))

    @pl.when(stage < stages - 1)
    def _():
        relay.start()

    z_copy = {
        k: remote(dense.at[0, 0], dense.at[k, 0], z_send.at[k], z_recv.at[k], at(x, y, z_partner(z, k)))
        for k in range(1, SIDE)
    }

    def d_copies(k):
        return {
            d: remote(dense.at[k, 0], dense.at[k, d], d_send.at[k, d], d_recv.at[k, d], along(inner[k], d))
            for d in near_hops(k)
        }

    def f_copies(k):
        return {
            d: remote(slots.at[k, d - 1], rows.at[k, d], f_send.at[k, d], f_recv.at[k, d], along(outer[k], d))
            for d in near_hops(k)
        }

    def rf_copies(k):
        return {
            d: remote(parts.at[k, d - 1], back.at[k, d], rf_send.at[k, d], rf_recv.at[k, d], along(outer[k], -d))
            for d in near_hops(k ^ 1)
        }

    def rd_copies(k):
        return {
            d: remote(merged.at[k, d], spread.at[k, d - 1], rd_send.at[k, d], rd_recv.at[k, d], along(inner[k], -d))
            for d in near_hops(k ^ 1)
        }

    def near_hops(k):
        return (2, 1, 3) if k % 2 == 0 else (1, 3)

    twin = at(x, y, z_partner(z, 1))

    def pair_copy(kind, src, dst, k):
        return {0: remote(src, dst, q_send.at[kind, k // 2], q_recv.at[kind, k // 2], twin)}

    rz_copy = {
        k: remote(sums.at[k], final.at[k], rz_send.at[k], rz_recv.at[k], at(x, y, z_partner(z, k)))
        for k in range(1, SIDE)
    }
    steps = {}

    def start(name, k, copies):
        steps[name, k] = copies
        for copy in copies.values():
            copy.start()

    def arrive(name, k, hops=None):
        for d, copy in steps[name, k].items():
            if hops is None or d in hops:
                copy.wait_recv()

    def lane_expert(k, lane):
        block = lane // BLOCK
        if outer[k] == "y":
            return 2 * x + ((y + block) % SIDE) // 2
        return 2 * ((x + block) % SIDE) + y // 2

    def prepare():
        values = inputs[...].astype(F32)
        mean_square = jnp.mean(values * values, axis=-1, keepdims=True)
        normed = (values * lax.rsqrt(mean_square + 1e-05) * gain_ref[...]).astype(BF16)
        dense[0, 0, :, pl.ds(0, width)] = normed
        logits = lax.dot_general(
            router_ref[...], normed, (((1,), (1,)), ((), ())), preferred_element_type=F32
        )
        ids = lax.broadcasted_iota(jnp.int32, (EXPERTS, TOK), 0)
        first, second = ids == routes_ref[0:1, :], ids == routes_ref[1:2, :]
        gap = jnp.sum(jnp.where(first, logits, 0.0), axis=0, keepdims=True) - jnp.sum(
            jnp.where(second, logits, 0.0), axis=0, keepdims=True
        )
        share_a, share_b = 1.0 / (1.0 + jnp.exp(-gap)), 1.0 / (1.0 + jnp.exp(gap))
        weight = jnp.where(first, share_a, 0.0) + jnp.where(second, share_b, 0.0)
        high = weight.astype(BF16).astype(F32)
        hit = jnp.where(first | second, 1.0, 0.0)
        here = lax.broadcasted_iota(jnp.int32, (TOK, TOK), 0)
        there = lax.broadcasted_iota(jnp.int32, (TOK, TOK), 1)
        upto = jnp.where(here <= there, 1.0, 0.0).astype(BF16)
        slot = hit * jnp.dot(hit.astype(BF16), upto, preferred_element_type=F32)
        table = jnp.concatenate(
            [slot, high, weight - high, jnp.zeros((META - 3 * EXPERTS, TOK), F32)], axis=0
        ).astype(BF16)
        same = jnp.where(here == there, 1.0, 0.0).astype(BF16)
        meta = lax.dot_general(same, table, (((1,), (1,)), ((), ())), preferred_element_type=F32)
        dense[0, 0, :, pl.ds(width, META)] = meta.astype(BF16)

    def compact(k):
        tok = dense[k].reshape(SIDE * TOK, width + META)
        meta = tok[:, width:]
        lane = lax.broadcasted_iota(jnp.int32, (SIDE * BLOCK, META), 0)
        col = lax.broadcasted_iota(jnp.int32, (SIDE * BLOCK, META), 1)
        pick = (col == lane_expert(k, lane)).astype(F32).astype(BF16)
        found = lax.dot_general(pick, meta, (((1,), (1,)), ((), ())), preferred_element_type=F32)
        lane = lax.broadcasted_iota(jnp.int32, (SIDE * BLOCK, SIDE * TOK), 0)
        token = lax.broadcasted_iota(jnp.int32, (SIDE * BLOCK, SIDE * TOK), 1)
        want = (lane % CAP + 1).astype(F32)
        near = (lane % BLOCK) // CAP == token // TOK
        placing = jnp.where((found == want) & near, 1.0, 0.0).astype(BF16)
        moved = jnp.dot(placing, tok[:, :width], preferred_element_type=F32).astype(BF16)
        rows[k, 0] = moved[:BLOCK]
        slots[k] = moved[BLOCK:].reshape(SIDE - 1, BLOCK, width)

    def experts(k):
        taken = rows[k].reshape(SIDE * BLOCK, width)

        def first(n, carry):
            cols = pl.ds(pl.multiple_of(n * 256, 256), 256)
            both = jnp.dot(taken, w_in[:, cols], preferred_element_type=F32)
            gate, up = both[:, :128], both[:, 128:]
            value = gate / (1.0 + jnp.exp(-gate)) * up
            hidden[:, pl.ds(pl.multiple_of(n * 128, 128), 128)] = value.astype(BF16)
            return carry

        lax.fori_loop(0, tiles, first, 0)

        def second(n, carry):
            cols = pl.ds(pl.multiple_of(n * 256, 256), 256)
            value = jnp.dot(hidden[...], w_out[:, cols], preferred_element_type=F32)
            back[k, 0, :, cols] = value[:BLOCK].astype(BF16)
            for d in range(1, SIDE):
                part = value[d * BLOCK : (d + 1) * BLOCK]
                if d == 2 and k % 2:
                    part = part + pair_parts[k // 2, :, cols].astype(F32)
                parts[k, d - 1, :, cols] = part.astype(BF16)
            return carry

        lax.fori_loop(0, width // 256, second, 0)

    def merge(k):
        meta = dense[k, :, :, pl.ds(width, META)].reshape(SIDE * TOK, META)
        col = lax.broadcasted_iota(jnp.int32, (META, SIDE * BLOCK), 0)
        lane = lax.broadcasted_iota(jnp.int32, (META, SIDE * BLOCK), 1)
        mine = lane_expert(k, lane)

        def look(shift):
            pick = (col == mine + shift).astype(F32).astype(BF16)
            return jnp.dot(meta, pick, preferred_element_type=F32)

        token = lax.broadcasted_iota(jnp.int32, (SIDE * TOK, SIDE * BLOCK), 0)
        lane = lax.broadcasted_iota(jnp.int32, (SIDE * TOK, SIDE * BLOCK), 1)
        want = (lane % CAP + 1).astype(F32)
        near = (lane % BLOCK) // CAP == token // TOK
        match = (look(0) == want) & near
        high = jnp.where(match, look(EXPERTS), 0.0).astype(BF16)
        low = jnp.where(match, look(2 * EXPERTS), 0.0).astype(BF16)
        came = back[k].reshape(SIDE * BLOCK, width)
        total = jnp.dot(high, came, preferred_element_type=F32) + jnp.dot(low, came, preferred_element_type=F32)
        for d in range(SIDE):
            part = total[d * TOK : (d + 1) * TOK]
            if d == 2 and k % 2:
                part = part + pair_merged[k // 2].astype(F32)
            merged[k, d] = part.astype(BF16)

    def gather_sum(k):
        total = merged[k, 0].astype(F32)
        for d in near_hops(k ^ 1):
            total = total + spread[k, d - 1].astype(F32)
        sums[k] = total.astype(BF16)

    weights = [pltpu.make_async_copy(down_ref, w_out, w_sem.at[2 * tiles])]
    for n in range(tiles):
        for j, ref in enumerate((gate_ref, up_ref)):
            weights.append(
                pltpu.make_async_copy(
                    ref.at[:, pl.ds(n * 128, 128)],
                    w_in.at[:, pl.ds(n * 256 + j * 128, 128)],
                    w_sem.at[2 * n + j],
                )
            )

    for copy in weights:
        copy.start()

    @pl.when(stage == 0)
    def _():
        inputs[...] = fresh_ref[...]

    @pl.when(stage > 0)
    def _():
        relay.wait_recv()

    prepare()
    start("d", 0, d_copies(0))
    for k in (2, 1, 3):
        start("z", k, {0: z_copy[k]})
    for k in (0, 2):
        back[k, 2] = jnp.zeros((BLOCK, width), BF16)

    def dense_on(k):
        arrive("z", k)
        start("d", k, d_copies(k))

    def dispatch(k):
        arrive("d", k, (2,))
        if k % 2 == 0:
            start("zd", k, pair_copy(0, dense.at[k, 2], dense.at[k + 1, 2], k))
        else:
            arrive("zd", k - 1)
        arrive("d", k, (1, 3))
        compact(k)
        start("f", k, f_copies(k))

    def pass_rows(k):
        arrive("f", k, (2,))
        start("zf", k, pair_copy(1, rows.at[k, 2], rows.at[k + 1, 2], k))

    def compute(k):
        arrive("f", k, (1, 3))
        if k % 2:
            arrive("zf", k - 1)
            arrive("zrf", k - 1)
        experts(k)
        if k % 2 == 0:
            start("zrf", k, pair_copy(2, parts.at[k, 1], pair_parts.at[k // 2], k))
        start("rf", k, rf_copies(k))

    def combine(k):
        arrive("rf", k)
        if k % 2:
            arrive("zrd", k - 1)
        merge(k)
        if k % 2 == 0:
            start("zrd", k, pair_copy(3, merged.at[k, 2], pair_merged.at[k // 2], k))
        start("rd", k, rd_copies(k))

    def collect(k):
        arrive("rd", k)
        gather_sum(k)
        if k:
            start("rz", k, {0: rz_copy[k]})

    dense_on(2)
    dispatch(0)
    dense_on(1)
    dispatch(2)
    dense_on(3)
    dispatch(1)
    dispatch(3)
    pass_rows(0)
    pass_rows(2)
    for copy in weights:
        copy.wait()
    compute(0)
    compute(2)
    compute(1)
    combine(0)
    compute(3)
    combine(2)
    combine(1)
    combine(3)
    collect(0)
    collect(2)
    collect(3)
    collect(1)
    total = inputs[...].astype(F32) + sums[0].astype(F32)
    for k in (2, 3, 1):
        arrive("rz", k)
        total = total + final[k].astype(F32)
    out_ref[...] = total.astype(BF16)
    for copies in steps.values():
        for copy in copies.values():
            copy.wait_send()

    @pl.when(stage < stages - 1)
    def _():
        relay.wait_send()


def run_layer(held, fresh, routes, gain, router, gate, up, down):
    tok, width = fresh.shape
    hid = gate.shape[1]
    vmem = pl.BlockSpec(memory_space=pltpu.VMEM)
    hbm = pl.BlockSpec(memory_space=pl.ANY)
    dma = pltpu.SemaphoreType.DMA
    pairs = [dma((SIDE,)), dma((SIDE,))]
    grids = [dma((SIDE, SIDE)), dma((SIDE, SIDE))]
    return pl.pallas_call(
        moe_kernel,
        out_shape=jax.ShapeDtypeStruct((tok, width), BF16),
        in_specs=[hbm, vmem, vmem, vmem, vmem, hbm, hbm, hbm],
        out_specs=vmem,
        scratch_shapes=[
            pltpu.VMEM((tok, width), BF16),
            pltpu.VMEM((SIDE, SIDE, tok, width + META), BF16),
            pltpu.VMEM((SIDE, SIDE - 1, BLOCK, width), BF16),
            pltpu.VMEM((SIDE, SIDE, BLOCK, width), BF16),
            pltpu.VMEM((SIDE, SIDE - 1, BLOCK, width), BF16),
            pltpu.VMEM((SIDE, SIDE, BLOCK, width), BF16),
            pltpu.VMEM((SIDE, SIDE, tok, width), BF16),
            pltpu.VMEM((SIDE, SIDE - 1, tok, width), BF16),
            pltpu.VMEM((SIDE, tok, width), BF16),
            pltpu.VMEM((SIDE, tok, width), BF16),
            pltpu.VMEM((2, BLOCK, width), BF16),
            pltpu.VMEM((2, tok, width), BF16),
            pltpu.VMEM((SIDE * BLOCK, hid), BF16),
            pltpu.VMEM((width, 2 * hid), BF16),
            pltpu.VMEM((hid, width), BF16),
        ]
        + pairs + grids + grids + grids + grids + pairs
        + grids + [dma((1,)), dma((1,)), dma((2 * (hid // 128) + 1,))],
        compiler_params=pltpu.CompilerParams(
            collective_id=0, has_side_effects=True, vmem_limit_bytes=60 * 1024 * 1024
        ),
        name="moe_relay",
    )(held, fresh, routes, gain, router, gate, up, down)


def per_device(held, fresh, routes, norm_gain, router, w_gate, w_up, w_down):
    out = run_layer(
        held[0], fresh, routes[0].T, norm_gain, router[0].T, w_gate[0, 0], w_up[0, 0], w_down[0, 0]
    )
    return out[None]


def solution(mesh):
    in_specs = (
        P("pipe", "expert", None),
        P("expert", None),
        P("pipe", "expert", None),
        P("pipe", None),
        P("pipe", None, None),
        P("pipe", "expert", None, None),
        P("pipe", "expert", None, None),
        P("pipe", "expert", None, None),
    )
    out_specs = P("pipe", "expert", None)
    return jax.shard_map(
        per_device, mesh=mesh, in_specs=in_specs, out_specs=out_specs, check_vma=False
    )
```

time: 111 us -> 99.1 us (0.89); the launches traced: 110 us -> 99 us
  starting transfers between devices: 10.3 us -> 0 us
  Pallas kernels: 92 us -> 97.4 us
  other arithmetic: 3.12 us -> 0 us
  waiting for transfers between devices: 1.33 us -> 0 us
    ppermute x1 -> x0, starting transfers between devices: 10.3 us -> none  [passed_along(): return lax.ppermute(x, axis, pairs)]
    pallas_call x1, Pallas kernels: 92 us -> 97.4 us  [run_layer(): pl.pallas_call(moe_kernel, out_shape=jax.ShapeDtypeStruct((tok, width), B...]
    reduce_sum x3 -> x0, other arithmetic: 1.56 us -> none  [the longest x1 0.71 us: per_device(): picked = jnp.sum(hits.astype(F32) * logits[:, None, :], axis=2)]
    ppermute x1 -> x0, waiting for transfers between devices: 1.33 us -> none  [passed_along(): return lax.ppermute(x, axis, pairs)]
  transfers between devices with their start and end apart: 1 -> 0, of which waited for: 1 -> 0; matrix products, arithmetic and copies ran while one was open for 1% -> 0% of each run, Pallas kernels for 0% -> 0%
where the time goes in v2:
time: 99.1 us; the launch traced here: 99 us
  Pallas kernels  97.4 us (98%)
  local copies, waits for them, and re-layouts  1.57 us (2%)
    pallas_call x1, Pallas kernels, run_layer(): pl.pallas_call(moe_kernel, out_shape=jax.ShapeDtypeStruct((tok, width), B...  97.4 us

profile of v2, /device:TPU:1, one launch (start us, length us, event | category | flops | bytes accessed | tf_op | source)
XLA Modules:
  0.0 99.0 jit_solution(9102303156205409746)
XLA Ops:
  0.0 97.4 %moe_relay.1 = bf16[32,2048]{1,0:T(8,128)(2,1)} custom-call(bf16[32,2048]{1,0:T(8,128)(2,1)} %bitcast.15, bf16[32,2048]{1,0:T(8,128)(2,1)} %fresh_ref.1, s32[2,32]{1,0:T(2,128)} %bitcast.17, f32[1,2048]{1,0:T(1,128)} %gain_ref.1, bf16[8,2048]{1,0:T(8,128)(2,1)} %bitcast.16, bf16[2048,896]{1,0:T(8,128)(2,1)} %bitcast.11, bf16[2048,896]{1,0:T(8,128)(2,1)} %bitcast.12, ...), custom_call_target="tpu_custom_call" | custom-call | tf_op jit(solution)/shard_map/moe_relay/pallas_call | solution.py:355
  97.4 1.6 %copy.10 = bf16[1,32,2048]{2,1,0:T(8,128)(2,1)} copy(bf16[1,32,2048]{2,1,0:T(8,128)(2,1)} %bitcast.14) | data formatting | bytes 262144

commit v3 on v2

--- a/solution.py
+++ b/solution.py
@@ -24,9 +24,9 @@
 
 def moe_kernel(
     held_ref, fresh_ref, routes_ref, gain_ref, router_ref, gate_ref, up_ref, down_ref, out_ref,
-    inputs, dense, slots, rows, parts, back, merged, spread, sums, final, pair_parts, pair_merged, hidden, w_in, w_out,
+    inputs, chosen, gain, router, dense, slots, rows, parts, back, merged, spread, sums, final, pair_parts, pair_merged, choice, hidden, w_in, w_out,
     z_send, z_recv, d_send, d_recv, f_send, f_recv,
-    rf_send, rf_recv, rd_send, rd_recv, rz_send, rz_recv, q_send, q_recv, p_send, p_recv, w_sem,
+    rf_send, rf_recv, rd_send, rd_recv, rz_send, rz_recv, q_send, q_recv, p_send, p_recv, i_sem, w_sem,
 ):
     me = lax.axis_index("expert")
     stage, stages = lax.axis_index("pipe"), lax.axis_size("pipe")
@@ -48,6 +48,18 @@
     def section(by):
         return {"pipe": stage + by, "expert": me}
 
+    loads = [
+        pltpu.make_async_copy(ref, to, i_sem.at[n])
+        for n, (ref, to) in enumerate(((routes_ref, chosen), (gain_ref, gain), (router_ref, router)))
+    ]
+    for copy in loads:
+        copy.start()
+    first_tile = pltpu.make_async_copy(fresh_ref, inputs, i_sem.at[3])
+
+    @pl.when(stage == 0)
+    def _():
+        first_tile.start()
+
     barrier = pltpu.get_barrier_semaphore()
 
     @pl.when(stage < stages - 1)
@@ -86,21 +98,34 @@
             for d in near_hops(k)
         }
 
-    def f_copies(k):
+    def f_copies(k, low, high):
+        span, lane = pl.ds(low * CAP, (high - low) * CAP), SIDE if low else 0
         return {
-            d: remote(slots.at[k, d - 1], rows.at[k, d], f_send.at[k, d], f_recv.at[k, d], along(outer[k], d))
+            d: remote(
+                slots.at[k, d - 1, span], rows.at[k, d, span],
+                f_send.at[k, lane + d], f_recv.at[k, lane + d], along(outer[k], d),
+            )
             for d in near_hops(k)
         }
 
-    def rf_copies(k):
+    def half(h):
+        return pl.ds(h * (width // 2), width // 2)
+
+    def rf_copies(k, h):
         return {
-            d: remote(parts.at[k, d - 1], back.at[k, d], rf_send.at[k, d], rf_recv.at[k, d], along(outer[k], -d))
+            d: remote(
+                parts.at[k, d - 1, :, half(h)], back.at[k, d, :, half(h)],
+                rf_send.at[k, h * SIDE + d], rf_recv.at[k, h * SIDE + d], along(outer[k], -d),
+            )
             for d in near_hops(k ^ 1)
         }
 
-    def rd_copies(k):
+    def rd_copies(k, h):
         return {
-            d: remote(merged.at[k, d], spread.at[k, d - 1], rd_send.at[k, d], rd_recv.at[k, d], along(inner[k], -d))
+            d: remote(
+                merged.at[k, d, :, half(h)], spread.at[k, d - 1, :, half(h)],
+                rd_send.at[k, h * SIDE + d], rd_recv.at[k, h * SIDE + d], along(inner[k], -d),
+            )
             for d in near_hops(k ^ 1)
         }
 
@@ -109,13 +134,16 @@
 
     twin = at(x, y, z_partner(z, 1))
 
-    def pair_copy(kind, src, dst, k):
-        return {0: remote(src, dst, q_send.at[kind, k // 2], q_recv.at[kind, k // 2], twin)}
-
-    rz_copy = {
-        k: remote(sums.at[k], final.at[k], rz_send.at[k], rz_recv.at[k], at(x, y, z_partner(z, k)))
-        for k in range(1, SIDE)
-    }
+    def pair_copy(kind, src, dst, k, h=0):
+        lane = h * SIDE + k // 2
+        return {0: remote(src, dst, q_send.at[kind, lane], q_recv.at[kind, lane], twin)}
+
+    def rz_copy(k, h):
+        return remote(
+            sums.at[k, :, half(h)], final.at[k, :, half(h)],
+            rz_send.at[k, h], rz_recv.at[k, h], at(x, y, z_partner(z, k)),
+        )
+
     steps = {}
 
     def start(name, k, copies):
@@ -128,8 +156,7 @@
             if hops is None or d in hops:
                 copy.wait_recv()
 
-    def lane_expert(k, lane):
-        block = lane // BLOCK
+    def lane_expert(k, block):
         if outer[k] == "y":
             return 2 * x + ((y + block) % SIDE) // 2
         return 2 * ((x + block) % SIDE) + y // 2
@@ -137,13 +164,13 @@
     def prepare():
         values = inputs[...].astype(F32)
         mean_square = jnp.mean(values * values, axis=-1, keepdims=True)
-        normed = (values * lax.rsqrt(mean_square + 1e-05) * gain_ref[...]).astype(BF16)
+        normed = (values * lax.rsqrt(mean_square + 1e-05) * gain[...]).astype(BF16)
         dense[0, 0, :, pl.ds(0, width)] = normed
         logits = lax.dot_general(
-            router_ref[...], normed, (((1,), (1,)), ((), ())), preferred_element_type=F32
+            router[...], normed, (((1,), (1,)), ((), ())), preferred_element_type=F32
         )
         ids = lax.broadcasted_iota(jnp.int32, (EXPERTS, TOK), 0)
-        first, second = ids == routes_ref[0:1, :], ids == routes_ref[1:2, :]
+        first, second = ids == chosen[0:1, :], ids == chosen[1:2, :]
         gap = jnp.sum(jnp.where(first, logits, 0.0), axis=0, keepdims=True) - jnp.sum(
             jnp.where(second, logits, 0.0), axis=0, keepdims=True
         )
@@ -162,26 +189,27 @@
         meta = lax.dot_general(same, table, (((1,), (1,)), ((), ())), preferred_element_type=F32)
         dense[0, 0, :, pl.ds(width, META)] = meta.astype(BF16)
 
-    def compact(k):
-        tok = dense[k].reshape(SIDE * TOK, width + META)
+    def compact(k, low, high):
+        count, span = high - low, (high - low) * CAP
+        tok = dense[k, low:high].reshape(count * TOK, width + META)
         meta = tok[:, width:]
-        lane = lax.broadcasted_iota(jnp.int32, (SIDE * BLOCK, META), 0)
-        col = lax.broadcasted_iota(jnp.int32, (SIDE * BLOCK, META), 1)
-        pick = (col == lane_expert(k, lane)).astype(F32).astype(BF16)
+        lane = lax.broadcasted_iota(jnp.int32, (SIDE * span, META), 0)
+        col = lax.broadcasted_iota(jnp.int32, (SIDE * span, META), 1)
+        pick = (col == lane_expert(k, lane // span)).astype(F32).astype(BF16)
         found = lax.dot_general(pick, meta, (((1,), (1,)), ((), ())), preferred_element_type=F32)
-        lane = lax.broadcasted_iota(jnp.int32, (SIDE * BLOCK, SIDE * TOK), 0)
-        token = lax.broadcasted_iota(jnp.int32, (SIDE * BLOCK, SIDE * TOK), 1)
+        lane = lax.broadcasted_iota(jnp.int32, (SIDE * span, count * TOK), 0)
+        token = lax.broadcasted_iota(jnp.int32, (SIDE * span, count * TOK), 1)
         want = (lane % CAP + 1).astype(F32)
-        near = (lane % BLOCK) // CAP == token // TOK
+        near = (lane % span) // CAP == token // TOK
         placing = jnp.where((found == want) & near, 1.0, 0.0).astype(BF16)
         moved = jnp.dot(placing, tok[:, :width], preferred_element_type=F32).astype(BF16)
-        rows[k, 0] = moved[:BLOCK]
-        slots[k] = moved[BLOCK:].reshape(SIDE - 1, BLOCK, width)
+        rows[k, 0, pl.ds(low * CAP, span)] = moved[:span]
+        for d in range(1, SIDE):
+            slots[k, d - 1, pl.ds(low * CAP, span)] = moved[d * span : (d + 1) * span]
 
     def experts(k):
-        taken = rows[k].reshape(SIDE * BLOCK, width)
-
         def first(n, carry):
+            taken = rows[k].reshape(SIDE * BLOCK, width)
             cols = pl.ds(pl.multiple_of(n * 256, 256), 256)
             both = jnp.dot(taken, w_in[:, cols], preferred_element_type=F32)
             gate, up = both[:, :128], both[:, 128:]
@@ -189,10 +217,11 @@
             hidden[:, pl.ds(pl.multiple_of(n * 128, 128), 128)] = value.astype(BF16)
             return carry
 
-        lax.fori_loop(0, tiles, first, 0)
-
+        lax.fori_loop(0, tiles, first, 0, unroll=True)
+
+    def project(k, h):
         def second(n, carry):
-            cols = pl.ds(pl.multiple_of(n * 256, 256), 256)
+            cols = pl.ds(h * (width // 2) + n * 256, 256)
             value = jnp.dot(hidden[...], w_out[:, cols], preferred_element_type=F32)
             back[k, 0, :, cols] = value[:BLOCK].astype(BF16)
             for d in range(1, SIDE):
@@ -202,13 +231,14 @@
                 parts[k, d - 1, :, cols] = part.astype(BF16)
             return carry
 
-        lax.fori_loop(0, width // 256, second, 0)
-
-    def merge(k):
+        for n in range(width // 512):
+            second(n, 0)
+
+    def choose(k):
         meta = dense[k, :, :, pl.ds(width, META)].reshape(SIDE * TOK, META)
         col = lax.broadcasted_iota(jnp.int32, (META, SIDE * BLOCK), 0)
         lane = lax.broadcasted_iota(jnp.int32, (META, SIDE * BLOCK), 1)
-        mine = lane_expert(k, lane)
+        mine = lane_expert(k, lane // BLOCK)
 
         def look(shift):
             pick = (col == mine + shift).astype(F32).astype(BF16)
@@ -221,19 +251,23 @@
         match = (look(0) == want) & near
         high = jnp.where(match, look(EXPERTS), 0.0).astype(BF16)
         low = jnp.where(match, look(2 * EXPERTS), 0.0).astype(BF16)
-        came = back[k].reshape(SIDE * BLOCK, width)
-        total = jnp.dot(high, came, preferred_element_type=F32) + jnp.dot(low, came, preferred_element_type=F32)
+        choice[k, 0], choice[k, 1] = high, low
+
+    def merge(k, h):
+        came = back[k, :, :, half(h)].reshape(SIDE * BLOCK, width // 2)
+        total = jnp.dot(choice[k, 0], came, preferred_element_type=F32)
+        total = total + jnp.dot(choice[k, 1], came, preferred_element_type=F32)
         for d in range(SIDE):
             part = total[d * TOK : (d + 1) * TOK]
             if d == 2 and k % 2:
-                part = part + pair_merged[k // 2].astype(F32)
-            merged[k, d] = part.astype(BF16)
-
-    def gather_sum(k):
-        total = merged[k, 0].astype(F32)
+                part = part + pair_merged[k // 2, :, half(h)].astype(F32)
+            merged[k, d, :, half(h)] = part.astype(BF16)
+
+    def gather_sum(k, h):
+        total = merged[k, 0, :, half(h)].astype(F32)
         for d in near_hops(k ^ 1):
-            total = total + spread[k, d - 1].astype(F32)
-        sums[k] = total.astype(BF16)
+            total = total + spread[k, d - 1, :, half(h)].astype(F32)
+        sums[k, :, half(h)] = total.astype(BF16)
 
     weights = [pltpu.make_async_copy(down_ref, w_out, w_sem.at[2 * tiles])]
     for n in range(tiles):
@@ -251,12 +285,14 @@
 
     @pl.when(stage == 0)
     def _():
-        inputs[...] = fresh_ref[...]
+        first_tile.wait()
 
     @pl.when(stage > 0)
     def _():
         relay.wait_recv()
 
+    for copy in loads:
+        copy.wait()
     prepare()
     start("d", 0, d_copies(0))
     for k in (2, 1, 3):
@@ -267,6 +303,10 @@
     def dense_on(k):
         arrive("z", k)
         start("d", k, d_copies(k))
+
+    def send_rows(k, low, high):
+        compact(k, low, high)
+        start("f", (k, low), f_copies(k, low, high))
 
     def dispatch(k):
         arrive("d", k, (2,))
@@ -275,66 +315,83 @@
         else:
             arrive("zd", k - 1)
         arrive("d", k, (1, 3))
-        compact(k)
-        start("f", k, f_copies(k))
+        send_rows(k, 1 if k % 2 == 0 else 0, SIDE)
+
+    def arrive_rows(k, hops):
+        arrive("f", (k, 0), hops)
+        if k % 2 == 0:
+            arrive("f", (k, 1), hops)
 
     def pass_rows(k):
-        arrive("f", k, (2,))
+        arrive_rows(k, (2,))
         start("zf", k, pair_copy(1, rows.at[k, 2], rows.at[k + 1, 2], k))
 
     def compute(k):
-        arrive("f", k, (1, 3))
+        arrive_rows(k, (1, 3))
         if k % 2:
             arrive("zf", k - 1)
-            arrive("zrf", k - 1)
         experts(k)
+        for h in range(2):
+            if k % 2:
+                arrive("zrf", (k - 1, h))
+            project(k, h)
+            if k % 2 == 0:
+                part, there = parts.at[k, 1, :, half(h)], pair_parts.at[k // 2, :, half(h)]
+                start("zrf", (k, h), pair_copy(2, part, there, k, h))
+            start("rf", (k, h), rf_copies(k, h))
+
+    def combine(k, h):
+        arrive("rf", (k, h))
+        if k % 2:
+            arrive("zrd", (k - 1, h))
+        merge(k, h)
         if k % 2 == 0:
-            start("zrf", k, pair_copy(2, parts.at[k, 1], pair_parts.at[k // 2], k))
-        start("rf", k, rf_copies(k))
-
-    def combine(k):
-        arrive("rf", k)
-        if k % 2:
-            arrive("zrd", k - 1)
-        merge(k)
-        if k % 2 == 0:
-            start("zrd", k, pair_copy(3, merged.at[k, 2], pair_merged.at[k // 2], k))
-        start("rd", k, rd_copies(k))
-
-    def collect(k):
-        arrive("rd", k)
-        gather_sum(k)
+            part, there = merged.at[k, 2, :, half(h)], pair_merged.at[k // 2, :, half(h)]
+            start("zrd", (k, h), pair_copy(3, part, there, k, h))
+        start("rd", (k, h), rd_copies(k, h))
+
+    def collect(k, h):
+        arrive("rd", (k, h))
+        gather_sum(k, h)
         if k:
-            start("rz", k, {0: rz_copy[k]})
-
+            start("rz", (k, h), {0: rz_copy(k, h)})
+
+    send_rows(0, 0, 1)
     dense_on(2)
+    send_rows(2, 0, 1)
+    dense_on(1)
     dispatch(0)
-    dense_on(1)
+    dense_on(3)
     dispatch(2)
-    dense_on(3)
     dispatch(1)
     dispatch(3)
-    pass_rows(0)
-    pass_rows(2)
+    for k in (0, 2, 1, 3):
+        choose(k)
     for copy in weights:
         copy.wait()
+    pass_rows(0)
     compute(0)
+    pass_rows(2)
     compute(2)
     compute(1)
-    combine(0)
+    combine(0, 0)
+    combine(0, 1)
     compute(3)
-    combine(2)
-    combine(1)
-    combine(3)
-    collect(0)
-    collect(2)
-    collect(3)
-    collect(1)
-    total = inputs[...].astype(F32) + sums[0].astype(F32)
-    for k in (2, 3, 1):
-        arrive("rz", k)
-        total = total + final[k].astype(F32)
-    out_ref[...] = total.astype(BF16)
+    combine(2, 0)
+    combine(2, 1)
+    combine(1, 0)
+    combine(3, 0)
+    combine(1, 1)
+    combine(3, 1)
+    for h in range(2):
+        for k in (0, 2, 3, 1):
+            collect(k, h)
+    for h in range(2):
+        total = inputs[:, half(h)].astype(F32) + sums[0, :, half(h)].astype(F32)
+        for k in (2, 3, 1):
+            arrive("rz", (k, h))
+            total = total + final[k, :, half(h)].astype(F32)
+        out_ref[:, half(h)] = total.astype(BF16)
     for copies in steps.values():
         for copy in copies.values():
             copy.wait_send()
@@ -348,17 +405,21 @@
     tok, width = fresh.shape
     hid = gate.shape[1]
     vmem = pl.BlockSpec(memory_space=pltpu.VMEM)
-    hbm = pl.BlockSpec(memory_space=pl.ANY)
+    hbm = pl.BlockSpec(memory_space=pltpu.MemorySpace.HBM)
     dma = pltpu.SemaphoreType.DMA
     pairs = [dma((SIDE,)), dma((SIDE,))]
+    wide = [dma((SIDE, 2 * SIDE)), dma((SIDE, 2 * SIDE))]
     grids = [dma((SIDE, SIDE)), dma((SIDE, SIDE))]
     return pl.pallas_call(
         moe_kernel,
         out_shape=jax.ShapeDtypeStruct((tok, width), BF16),
-        in_specs=[hbm, vmem, vmem, vmem, vmem, hbm, hbm, hbm],
+        in_specs=[hbm] * 8,
         out_specs=vmem,
         scratch_shapes=[
             pltpu.VMEM((tok, width), BF16),
+            pltpu.VMEM(routes.shape, jnp.int32),
+            pltpu.VMEM(gain.shape, F32),
+            pltpu.VMEM(router.shape, BF16),
             pltpu.VMEM((SIDE, SIDE, tok, width + META), BF16),
             pltpu.VMEM((SIDE, SIDE - 1, BLOCK, width), BF16),
             pltpu.VMEM((SIDE, SIDE, BLOCK, width), BF16),
@@ -370,14 +431,15 @@
             pltpu.VMEM((SIDE, tok, width), BF16),
             pltpu.VMEM((2, BLOCK, width), BF16),
             pltpu.VMEM((2, tok, width), BF16),
+            pltpu.VMEM((SIDE, 2, SIDE * tok, SIDE * BLOCK), BF16),
             pltpu.VMEM((SIDE * BLOCK, hid), BF16),
             pltpu.VMEM((width, 2 * hid), BF16),
             pltpu.VMEM((hid, width), BF16),
         ]
-        + pairs + grids + grids + grids + grids + pairs
-        + grids + [dma((1,)), dma((1,)), dma((2 * (hid // 128) + 1,))],
+        + pairs + grids + wide + wide + wide + grids
+        + wide + [dma((1,)), dma((1,)), dma((SIDE,)), dma((2 * (hid // 128) + 1,))],
         compiler_params=pltpu.CompilerParams(
-            collective_id=0, has_side_effects=True, vmem_limit_bytes=60 * 1024 * 1024
+            collective_id=0, has_side_effects=True, vmem_limit_bytes=58 * 1024 * 1024
         ),
         name="moe_relay",
     )(held, fresh, routes, gain, router, gate, up, down)

time: 99.1 us -> 85.6 us (0.86)
  Pallas kernels: 97.4 us -> 84 us
    pallas_call x1, Pallas kernels: 97.4 us -> 84 us  [run_layer(): pl.pallas_call(moe_kernel, out_shape=jax.ShapeDtypeStruct((tok, width), B...]
where the time goes in v3:
time: 85.6 us
  Pallas kernels  84 us (98%)
  local copies, waits for them, and re-layouts  1.57 us (2%)
    pallas_call x1, Pallas kernels, run_layer(): pl.pallas_call(moe_kernel, out_shape=jax.ShapeDtypeStruct((tok, width), B...  84 us

profile of v3, /device:TPU:1, one launch (start us, length us, event | category | flops | bytes accessed | tf_op | source)
XLA Modules:
  0.0 85.6 jit_solution(5201335244801593217)
XLA Ops:
  0.0 84.0 %moe_relay.1 = bf16[32,2048]{1,0:T(8,128)(2,1)} custom-call(bf16[32,2048]{1,0:T(8,128)(2,1)} %bitcast.15, bf16[32,2048]{1,0:T(8,128)(2,1)} %fresh_ref.1, s32[2,32]{1,0:T(2,128)} %bitcast.17, f32[1,2048]{1,0:T(1,128)} %gain_ref.1, bf16[8,2048]{1,0:T(8,128)(2,1)} %bitcast.16, bf16[2048,896]{1,0:T(8,128)(2,1)} %bitcast.11, bf16[2048,896]{1,0:T(8,128)(2,1)} %bitcast.12, ...), custom_call_target="tpu_custom_call" | custom-call | tf_op jit(solution)/shard_map/moe_relay/pallas_call | solution.py:413
  84.0 1.6 %copy.10 = bf16[1,32,2048]{2,1,0:T(8,128)(2,1)} copy(bf16[1,32,2048]{2,1,0:T(8,128)(2,1)} %bitcast.14) | data formatting | bytes 262144

commit v4 on v3

--- a/solution.py
+++ b/solution.py
@@ -89,7 +89,7 @@
 
     z_copy = {
         k: remote(dense.at[0, 0], dense.at[k, 0], z_send.at[k], z_recv.at[k], at(x, y, z_partner(z, k)))
-        for k in range(1, SIDE)
+        for k in (1, 2)
     }
 
     def d_copies(k):
@@ -295,13 +295,15 @@
         copy.wait()
     prepare()
     start("d", 0, d_copies(0))
-    for k in (2, 1, 3):
+    for k in (2, 1):
         start("z", k, {0: z_copy[k]})
     for k in (0, 2):
         back[k, 2] = jnp.zeros((BLOCK, width), BF16)
 
     def dense_on(k):
         arrive("z", k)
+        if k == 2:
+            start("z", 3, {0: remote(dense.at[2, 0], dense.at[3, 0], z_send.at[3], z_recv.at[3], twin)})
         start("d", k, d_copies(k))
 
     def send_rows(k, low, high):
@@ -358,15 +360,16 @@
 
     send_rows(0, 0, 1)
     dense_on(2)
+    dense_on(1)
     send_rows(2, 0, 1)
-    dense_on(1)
+    dense_on(3)
     dispatch(0)
-    dense_on(3)
+    choose(0)
     dispatch(2)
+    choose(2)
     dispatch(1)
+    choose(1)
     dispatch(3)
-    for k in (0, 2, 1, 3):
-        choose(k)
     for copy in weights:
         copy.wait()
     pass_rows(0)
@@ -374,6 +377,7 @@
     pass_rows(2)
     compute(2)
     compute(1)
+    choose(3)
     combine(0, 0)
     combine(0, 1)
     compute(3)
@@ -381,11 +385,15 @@
     combine(2, 1)
     combine(1, 0)
     combine(3, 0)
+    collect(2, 0)
+    collect(2, 1)
     combine(1, 1)
     combine(3, 1)
+    collect(0, 0)
+    collect(0, 1)
     for h in range(2):
-        for k in (0, 2, 3, 1):
-            collect(k, h)
+        collect(3, h)
+        collect(1, h)
     for h in range(2):
         total = inputs[:, half(h)].astype(F32) + sums[0, :, half(h)].astype(F32)
         for k in (2, 3, 1):

time: 85.6 us -> 82.9 us (0.968)
  Pallas kernels: 84 us -> 81.2 us
    pallas_call x1, Pallas kernels: 84 us -> 81.2 us  [run_layer(): pl.pallas_call(moe_kernel, out_shape=jax.ShapeDtypeStruct((tok, width), B...]
where the time goes in v4:
time: 82.9 us; the launch traced here: 82.8 us
  Pallas kernels  81.2 us (98%)
  local copies, waits for them, and re-layouts  1.57 us (2%)
    pallas_call x1, Pallas kernels, run_layer(): pl.pallas_call(moe_kernel, out_shape=jax.ShapeDtypeStruct((tok, width), B...  81.2 us

profile of v4, /device:TPU:1, one launch (start us, length us, event | category | flops | bytes accessed | tf_op | source)
XLA Modules:
  0.0 82.8 jit_solution(16662410681192094955)
XLA Ops:
  0.0 81.2 %moe_relay.1 = bf16[32,2048]{1,0:T(8,128)(2,1)} custom-call(bf16[32,2048]{1,0:T(8,128)(2,1)} %bitcast.15, bf16[32,2048]{1,0:T(8,128)(2,1)} %fresh_ref.1, s32[2,32]{1,0:T(2,128)} %bitcast.17, f32[1,2048]{1,0:T(1,128)} %gain_ref.1, bf16[8,2048]{1,0:T(8,128)(2,1)} %bitcast.16, bf16[2048,896]{1,0:T(8,128)(2,1)} %bitcast.11, bf16[2048,896]{1,0:T(8,128)(2,1)} %bitcast.12, ...), custom_call_target="tpu_custom_call" | custom-call | tf_op jit(solution)/shard_map/moe_relay/pallas_call | solution.py:421
  81.3 1.6 %copy.10 = bf16[1,32,2048]{2,1,0:T(8,128)(2,1)} copy(bf16[1,32,2048]{2,1,0:T(8,128)(2,1)} %bitcast.14) | data formatting | bytes 262144

commit v5 on v4

--- a/solution.py
+++ b/solution.py
@@ -24,9 +24,9 @@
 
 def moe_kernel(
     held_ref, fresh_ref, routes_ref, gain_ref, router_ref, gate_ref, up_ref, down_ref, out_ref,
-    inputs, chosen, gain, router, dense, slots, rows, parts, back, merged, spread, sums, final, pair_parts, pair_merged, choice, hidden, w_in, w_out,
+    inputs, result, chosen, gain, router, dense, slots, rows, parts, back, merged, spread, sums, final, pair_parts, pair_merged, choice, hidden, w_in, w_out,
     z_send, z_recv, d_send, d_recv, f_send, f_recv,
-    rf_send, rf_recv, rd_send, rd_recv, rz_send, rz_recv, q_send, q_recv, p_send, p_recv, i_sem, w_sem,
+    rf_send, rf_recv, rd_send, rd_recv, rz_send, rz_recv, q_send, q_recv, p_send, p_recv, o_sem, i_sem, w_sem,
 ):
     me = lax.axis_index("expert")
     stage, stages = lax.axis_index("pipe"), lax.axis_size("pipe")
@@ -280,9 +280,6 @@
                 )
             )
 
-    for copy in weights:
-        copy.start()
-
     @pl.when(stage == 0)
     def _():
         first_tile.wait()
@@ -359,6 +356,8 @@
             start("rz", (k, h), {0: rz_copy(k, h)})
 
     send_rows(0, 0, 1)
+    for copy in weights:
+        copy.start()
     dense_on(2)
     dense_on(1)
     send_rows(2, 0, 1)
@@ -384,25 +383,30 @@
     combine(2, 0)
     combine(2, 1)
     combine(1, 0)
+    combine(1, 1)
     combine(3, 0)
     collect(2, 0)
     collect(2, 1)
-    combine(1, 1)
     combine(3, 1)
     collect(0, 0)
     collect(0, 1)
     for h in range(2):
         collect(3, h)
         collect(1, h)
+    outputs = []
     for h in range(2):
         total = inputs[:, half(h)].astype(F32) + sums[0, :, half(h)].astype(F32)
         for k in (2, 3, 1):
             arrive("rz", (k, h))
             total = total + final[k, :, half(h)].astype(F32)
-        out_ref[:, half(h)] = total.astype(BF16)
+        result[:, half(h)] = total.astype(BF16)
+        outputs.append(pltpu.make_async_copy(result.at[:, half(h)], out_ref.at[:, half(h)], o_sem.at[h]))
+        outputs[h].start()
     for copies in steps.values():
         for copy in copies.values():
             copy.wait_send()
+    for copy in outputs:
+        copy.wait()
 
     @pl.when(stage < stages - 1)
     def _():
@@ -412,7 +416,6 @@
 def run_layer(held, fresh, routes, gain, router, gate, up, down):
     tok, width = fresh.shape
     hid = gate.shape[1]
-    vmem = pl.BlockSpec(memory_space=pltpu.VMEM)
     hbm = pl.BlockSpec(memory_space=pltpu.MemorySpace.HBM)
     dma = pltpu.SemaphoreType.DMA
     pairs = [dma((SIDE,)), dma((SIDE,))]
@@ -422,8 +425,9 @@
         moe_kernel,
         out_shape=jax.ShapeDtypeStruct((tok, width), BF16),
         in_specs=[hbm] * 8,
-        out_specs=vmem,
+        out_specs=hbm,
         scratch_shapes=[
+            pltpu.VMEM((tok, width), BF16),
             pltpu.VMEM((tok, width), BF16),
             pltpu.VMEM(routes.shape, jnp.int32),
             pltpu.VMEM(gain.shape, F32),
@@ -445,7 +449,7 @@
             pltpu.VMEM((hid, width), BF16),
         ]
         + pairs + grids + wide + wide + wide + grids
-        + wide + [dma((1,)), dma((1,)), dma((SIDE,)), dma((2 * (hid // 128) + 1,))],
+        + wide + [dma((1,)), dma((1,)), dma((2,)), dma((SIDE,)), dma((2 * (hid // 128) + 1,))],
         compiler_params=pltpu.CompilerParams(
             collective_id=0, has_side_effects=True, vmem_limit_bytes=58 * 1024 * 1024
         ),

time: 82.9 us -> 82.9 us (level)
  no operation moved by 1% of the time
where the time goes in v5:
time: 82.9 us; the launch traced here: 82.8 us
  Pallas kernels  81.2 us (98%)
  local copies, waits for them, and re-layouts  1.57 us (2%)
    pallas_call x1, Pallas kernels, run_layer(): pl.pallas_call(moe_kernel, out_shape=jax.ShapeDtypeStruct((tok, width), B...  81.2 us

profile of v5, /device:TPU:1, one launch (start us, length us, event | category | flops | bytes accessed | tf_op | source)
XLA Modules:
  0.0 82.8 jit_solution(8482298532203357890)
XLA Ops:
  0.0 81.2 %moe_relay.1 = bf16[32,2048]{1,0:T(8,128)(2,1)} custom-call(bf16[32,2048]{1,0:T(8,128)(2,1)} %bitcast.15, bf16[32,2048]{1,0:T(8,128)(2,1)} %fresh_ref.1, s32[2,32]{1,0:T(2,128)} %bitcast.17, f32[1,2048]{1,0:T(1,128)} %gain_ref.1, bf16[8,2048]{1,0:T(8,128)(2,1)} %bitcast.16, bf16[2048,896]{1,0:T(8,128)(2,1)} %bitcast.11, bf16[2048,896]{1,0:T(8,128)(2,1)} %bitcast.12, ...), custom_call_target="tpu_custom_call" | custom-call | tf_op jit(solution)/shard_map/moe_relay/pallas_call | solution.py:424
  81.2 1.6 %copy.10 = bf16[1,32,2048]{2,1,0:T(8,128)(2,1)} copy(bf16[1,32,2048]{2,1,0:T(8,128)(2,1)} %bitcast.14) | data formatting | bytes 262144

commit v6 on v5

--- a/solution.py
+++ b/solution.py
@@ -141,7 +141,7 @@
     def rz_copy(k, h):
         return remote(
             sums.at[k, :, half(h)], final.at[k, :, half(h)],
-            rz_send.at[k, h], rz_recv.at[k, h], at(x, y, z_partner(z, k)),
+            rz_send.at[k, h], rz_recv.at[k, h], twin if k == 2 else at(x, y, z_partner(z, k)),
         )
 
     steps = {}
@@ -267,6 +267,8 @@
         total = merged[k, 0, :, half(h)].astype(F32)
         for d in near_hops(k ^ 1):
             total = total + spread[k, d - 1, :, half(h)].astype(F32)
+        if k == 3:
+            total = total + final[2, :, half(h)].astype(F32)
         sums[k, :, half(h)] = total.astype(BF16)
 
     weights = [pltpu.make_async_copy(down_ref, w_out, w_sem.at[2 * tiles])]
@@ -351,6 +353,8 @@
 
     def collect(k, h):
         arrive("rd", (k, h))
+        if k == 3:
+            arrive("rz", (2, h))
         gather_sum(k, h)
         if k:
             start("rz", (k, h), {0: rz_copy(k, h)})
@@ -396,7 +400,7 @@
     outputs = []
     for h in range(2):
         total = inputs[:, half(h)].astype(F32) + sums[0, :, half(h)].astype(F32)
-        for k in (2, 3, 1):
+        for k in (3, 1):
             arrive("rz", (k, h))
             total = total + final[k, :, half(h)].astype(F32)
         result[:, half(h)] = total.astype(BF16)

time: 82.9 us -> 82.9 us (level)
  no operation moved by 1% of the time
where the time goes in v6:
time: 82.9 us; the launch traced here: 82.8 us
  Pallas kernels  81.2 us (98%)
  local copies, waits for them, and re-layouts  1.57 us (2%)
    pallas_call x1, Pallas kernels, run_layer(): pl.pallas_call(moe_kernel, out_shape=jax.ShapeDtypeStruct((tok, width), B...  81.2 us

profile of v6, /device:TPU:1, one launch (start us, length us, event | category | flops | bytes accessed | tf_op | source)
XLA Modules:
  0.0 82.8 jit_solution(1817748301535210915)
XLA Ops:
  0.0 81.2 %moe_relay.1 = bf16[32,2048]{1,0:T(8,128)(2,1)} custom-call(bf16[32,2048]{1,0:T(8,128)(2,1)} %bitcast.15, bf16[32,2048]{1,0:T(8,128)(2,1)} %fresh_ref.1, s32[2,32]{1,0:T(2,128)} %bitcast.17, f32[1,2048]{1,0:T(1,128)} %gain_ref.1, bf16[8,2048]{1,0:T(8,128)(2,1)} %bitcast.16, bf16[2048,896]{1,0:T(8,128)(2,1)} %bitcast.11, bf16[2048,896]{1,0:T(8,128)(2,1)} %bitcast.12, ...), custom_call_target="tpu_custom_call" | custom-call | tf_op jit(solution)/shard_map/moe_relay/pallas_call | solution.py:428
  81.2 1.6 %copy.10 = bf16[1,32,2048]{2,1,0:T(8,128)(2,1)} copy(bf16[1,32,2048]{2,1,0:T(8,128)(2,1)} %bitcast.14) | data formatting | bytes 262144
